TPU v7x, 32 devices: a whole 2x2x4 slice. The times are simulated.
32 devices in a mesh: frag: 4 (over y, core), band: 8 (over z, x).
Axes of the slice: x: 2, y: 2, z: 4, core: 2. Of those that a mesh axis runs over, the one named last changes fastest.
Arguments:
- wave_coeffs: bfloat16 [4, 256, 262144], P('frag', 'band'), may hold values from -40 to 40
- old_potential: float32 [4, 262144], P('frag'), may hold values from -4 to 4
- occupations: float32 [4, 256], P('frag'), may hold values from 0 to 2
- box_sizes: int32 [4, 3], replicated, may hold values from 32 to 64, as said below
- box_offsets: int32 [4, 3], replicated, may hold values from 0 to 96, as said below
- patch_signs: int32 [4], replicated, may hold values from -1 to 1, as said below
Outputs:
- new_waves: bfloat16 [4, 256, 262144], P('frag', 'band')
- box_potential: float32 [4, 262144], P('frag')
- total_potential: float32 [128, 128, 128], P('band')
Inputs may be any that keep to these rules, and one draw needn't show every extreme that they name: `box_sizes`: each entry is 32, 48 or 64. box_offsets + box_sizes <= 128 in every dimension. `patch_signs`: each entry is -1 or 1.
All inputs are finite; a program needn't handle non-finite values.
Results may differ from a plain program's by a relative error of at most 0.0065.
Values may be sent and summed in bfloat16 or wider, within the bound.
A program may use at most 384 MiB of HBM per device.

v0:
```python
import jax
import jax.numpy as jnp
from jax import lax
from jax.sharding import PartitionSpec as P

NB = 256
BOX = 64
G = 128
NS_ITERS = 8


step_size = 0.1
screening = 0.5
local_factor = 0.75
epsilon = 1e-06


def sine_table():
    index = jnp.arange(G).astype(jnp.float32) + 1.0
    table = jnp.sqrt(2.0 / (G + 1)) * jnp.sin(jnp.pi * index[:, None] * index[None, :] / (G + 1))
    eigen = 2.0 - 2.0 * jnp.cos(jnp.pi * index / (G + 1))
    return (table, eigen)


def newton_schulz(gram):
    highest = lax.Precision.HIGHEST
    frobenius = jnp.sqrt(jnp.sum(gram * gram) + epsilon)
    identity = jnp.eye(NB, dtype=jnp.float32)
    square_part = gram / frobenius
    inverse_part = identity
    for sweep in range(NS_ITERS):
        newton_step = 0.5 * (
            3.0 * identity
            - jnp.dot(
                inverse_part, square_part, precision=highest, preferred_element_type=jnp.float32
            )
        )
        square_part = jnp.dot(
            square_part, newton_step, precision=highest, preferred_element_type=jnp.float32
        )
        inverse_part = jnp.dot(
            newton_step, inverse_part, precision=highest, preferred_element_type=jnp.float32
        )
    return (inverse_part / jnp.sqrt(frobenius)).astype(jnp.bfloat16)


def shifted(field, offset):
    if offset > 0:
        tail = jnp.zeros((field.shape[0], offset), field.dtype)
        return jnp.concatenate([field[:, offset:], tail], axis=1)
    head = jnp.zeros((field.shape[0], -offset), field.dtype)
    return jnp.concatenate([head, field[:, :offset]], axis=1)


def body(wave_coeffs, old_potential, occupations, box_sizes, box_offsets, patch_signs):
    highest = lax.Precision.HIGHEST
    fragment = lax.axis_index("frag")
    band_index = lax.axis_index("band")
    band_count = lax.axis_size("band")
    cells = BOX * BOX * BOX
    cell_volume = 1.0 / BOX**3
    zero_index = jnp.zeros((), jnp.int32)
    sizes_here = lax.dynamic_index_in_dim(box_sizes, fragment, 0, keepdims=False)
    offsets_here = lax.dynamic_index_in_dim(box_offsets, fragment, 0, keepdims=False)
    sign_here = lax.dynamic_index_in_dim(patch_signs, fragment, 0, keepdims=False)
    position = jnp.arange(cells)
    x_coord = position // (BOX * BOX)
    y_coord = position // BOX % BOX
    z_coord = position % BOX
    mask = (
        (x_coord < sizes_here[0]) & (y_coord < sizes_here[1]) & (z_coord < sizes_here[2])
    ).astype(jnp.float32)
    waves = wave_coeffs[0].astype(jnp.float32) * mask[None, :]
    beside = shifted(waves, 1) * (z_coord < BOX - 1).astype(jnp.float32)[None, :]
    beside = beside + shifted(waves, -1) * (z_coord > 0).astype(jnp.float32)[None, :]
    beside = beside + shifted(waves, BOX) * (y_coord < BOX - 1).astype(jnp.float32)[None, :]
    beside = beside + shifted(waves, -BOX) * (y_coord > 0).astype(jnp.float32)[None, :]
    beside = beside + shifted(waves, BOX * BOX) * (x_coord < BOX - 1).astype(jnp.float32)[None, :]
    beside = beside + shifted(waves, -BOX * BOX) * (x_coord > 0).astype(jnp.float32)[None, :]
    kinetic = 6.0 * waves - beside
    applied = 0.5 * kinetic + old_potential[0][None, :] * waves
    trial = (mask[None, :] * (waves - step_size * applied)).astype(jnp.bfloat16)
    cell_rows = lax.all_to_all(trial, "band", split_axis=1, concat_axis=0, tiled=True)
    partial_value = lax.dot_general(
        cell_rows, cell_rows, (((1,), (1,)), ((), ())), preferred_element_type=jnp.float32
    )
    gram = lax.psum(partial_value, "band") * cell_volume
    coeff = newton_schulz(gram)
    fresh = lax.dot_general(
        coeff, cell_rows, (((0,), (0,)), ((), ())), preferred_element_type=jnp.float32
    )
    waves_out = lax.all_to_all(
        fresh.astype(jnp.bfloat16), "band", split_axis=0, concat_axis=1, tiled=True
    )
    density = jnp.sum(occupations[0][:, None] * fresh * fresh, axis=0) / NB
    slab_rows = G // band_count
    slab_start = band_index * slab_rows
    whole_box = lax.all_gather(density.astype(jnp.bfloat16), "band", axis=0, tiled=True).astype(
        density.dtype
    )
    padded_x = jnp.pad(whole_box.reshape(BOX, BOX, BOX), ((G, G), (0, 0), (0, 0)))
    planes = lax.dynamic_slice_in_dim(padded_x, slab_start - offsets_here[0] + G, slab_rows, 0)
    frame = jnp.zeros((slab_rows, G + BOX, G + BOX), jnp.float32)
    frame = lax.dynamic_update_slice(frame, planes, (zero_index, offsets_here[1], offsets_here[2]))
    mine = sign_here.astype(jnp.float32) * frame[:, :G, :G]
    patched = lax.psum(mine.astype(jnp.bfloat16), "frag").astype(jnp.float32)
    table, eigen = sine_table()
    spectrum = jnp.einsum("abc,ci->abi", patched, table, precision=highest)
    spectrum = jnp.einsum("abc,bi->aic", spectrum, table, precision=highest)
    columns = lax.all_to_all(
        spectrum.astype(jnp.bfloat16), "band", split_axis=1, concat_axis=0, tiled=True
    ).astype(spectrum.dtype)
    column_count = G // band_count
    eigen_y = lax.dynamic_slice_in_dim(eigen, band_index * column_count, column_count)
    columns = jnp.einsum("abc,ai->ibc", columns, table, precision=highest)
    columns = columns * (
        screening
        / (eigen[:, None, None] + eigen_y[None, :, None] + eigen[None, None, :] + screening)
    )
    columns = jnp.einsum("abc,ai->ibc", columns, table, precision=highest)
    slab = lax.all_to_all(columns, "band", split_axis=0, concat_axis=1, tiled=True)
    slab = jnp.einsum("abc,bi->aic", slab, table, precision=highest)
    hartree = jnp.einsum("abc,ci->abi", slab, table, precision=highest)
    total_potential = hartree - local_factor * jnp.cbrt(jnp.maximum(patched, 0.0))
    grid = lax.all_gather(total_potential.astype(jnp.bfloat16), "band", axis=0, tiled=True).astype(
        total_potential.dtype
    )
    extended = jnp.pad(grid, ((0, BOX), (0, BOX), (0, BOX)))
    window = lax.dynamic_slice(
        extended, (offsets_here[0], offsets_here[1], offsets_here[2]), (BOX, BOX, BOX)
    )
    box_potential = (window.reshape(cells) * mask)[None, :]
    return (waves_out[None], box_potential, total_potential)


def solution(mesh):
    placed = (P("frag", "band", None), P("frag", None), P("frag", None), P(), P(), P())
    return jax.shard_map(
        body,
        mesh=mesh,
        in_specs=placed,
        out_specs=(P("frag", "band", None), P("frag", None), P("band", None, None)),
        check_vma=False,
    )
```

profile of v0, /device:TPU:0, one launch (start us, length us, event | category | flops | bytes accessed | tf_op | source)
XLA Modules:
  0.0 1328.3 jit_solution(876237129467702302)
XLA Ops:
  7.2 1.3 constant_dynamic-slice_fusion
  8.5 0.7 fusion.89
  9.2 2.4 fusion.30
  11.6 18.2 %convert_multiply_fusion = f32[32,262144]{1,0:T(8,128)} fusion(bf16[1,32,262144]{2,1,0:T(8,128)(2,1)} %param.6, f32[262144]{0:T(1024)S(1)} %fusion.30), kind=kLoop, calls=%fused_computation.2 | loop fusion | flops 16777216 | bytes 51380224 | tf_op jit(solution)/shard_map/mul | solution.py:73
  29.8 44.2 %fusion.85 = (f32[32,262143]{1,0:T(8,128)}, f32[32,262143]{1,0:T(8,128)}) fusion(f32[32,262144]{1,0:T(8,128)} %convert_multiply_fusion), kind=kLoop, calls=%fused_computation.141 | loop fusion | bytes 134217216 | tf_op jit(solution)/shard_map/slice | solution.py:50
  74.0 44.3 %fusion.86 = (f32[32,262080]{1,0:T(8,128)}, f32[32,262080]{1,0:T(8,128)}) fusion(f32[32,262144]{1,0:T(8,128)} %convert_multiply_fusion), kind=kLoop, calls=%fused_computation.142 | loop fusion | bytes 134184960 | tf_op jit(solution)/shard_map/slice | solution.py:50
  118.3 43.3 %fusion.87 = (f32[32,258048]{1,0:T(8,128)}, f32[32,258048]{1,0:T(8,128)}) fusion(f32[32,262144]{1,0:T(8,128)} %convert_multiply_fusion), kind=kLoop, calls=%fused_computation.143 | loop fusion | bytes 132120576 | tf_op jit(solution)/shard_map/slice | solution.py:50
  161.7 1.6 fusion.33
  163.3 1.5 compare_convert_fusion
  164.8 74.9 %multiply_convert_fusion = bf16[32,262144]{1,0:T(8,128)(2,1)} fusion(f32[32,258048]{1,0:T(8,128)} %get-tuple-element.10, f32[32,258048]{1,0:T(8,128)} %get-tuple-element.9, f32[32,262080]{1,0:T(8,128)} %get-tuple-element.8, f32[32,262080]{1,0:T(8,128)} %get-tuple-element.7, f32[32,262143]{1,0:T(8,128)} %get-tuple-element.6, ...), kind=kLoop, calls=%fused_computation.3 | loop fusion | flops 184549376 | bytes 242204416 | tf_op jit(solution)/shard_map/convert_element_type | solution.py:82
  239.7 8.0 copy.60
  247.6 370.0 %all_to_all.71 = bf16[32,8,32768]{2,0,1:T(8,128)(2,1)} all-to-all(bf16[32,8,32768]{2,0,1:T(8,128)(2,1)S(1)} %bitcast.105), channel_id=1, replica_groups=mesh['frag'=4,'band'=8] {'band'}, dimensions={1} | all-to-all | bytes 33554432 | tf_op jit(solution)/shard_map/all_to_all | solution.py:83
  617.6 13.6 %fusion.91 = f32[256,256]{1,0:T(8,128)} fusion(bf16[256,32768]{1,0:T(8,128)(2,1)} %bitcast.108), kind=kOutput, calls=%fused_computation.147 | convolution fusion | flops 4294967296 | bytes 17039360 | tf_op jit(solution)/shard_map/dot_general | solution.py:84
  631.5 0.6 fusion.88
  635.3 0.7 dynamic_slice.21
  638.0 63.6 %all-reduce.11.cloned.1.call-done = f32[256,256]{1,0:T(8,128)} async-done(((f32[256,256]{1,0:T(8,128)}), f32[256,256]{1,0:T(8,128)}) %all-reduce.11.cloned.1.call-update) | async-done | bytes 262160 | tf_op jit(solution)/shard_map/psum | solution.py:87
  701.5 1.6 multiply_reduce_fusion
  703.9 1.3 fusion.14
  705.4 1.3 fusion.38
  706.8 0.4 fusion.13
  707.1 0.4 fusion.93
  707.5 0.4 fusion.92
  707.9 0.4 fusion.12
  708.3 0.4 fusion.95
  708.7 0.4 fusion.94
  709.1 0.4 fusion.11
  709.5 0.4 fusion.97
  709.9 0.4 fusion.96
  710.2 0.4 fusion.10
  710.6 0.4 fusion.99
  711.0 0.4 fusion.98
  711.4 0.4 fusion.9
  711.8 0.4 fusion.101
  712.2 0.4 fusion.100
  712.6 0.4 fusion.8
  713.0 0.4 fusion.103
  713.8 0.4 fusion.7
  714.2 0.4 fusion.15
  714.6 16.2 %fusion = (f32[32768]{0:T(1024)S(1)}, bf16[256,32768]{1,0:T(8,128)(2,1)}) fusion(f32[256]{0:T(256)S(1)} %bitcast.115, bf16[256,256]{1,0:T(8,128)(2,1)S(1)} %fusion.15, bf16[256,32768]{1,0:T(8,128)(2,1)} %bitcast.109), kind=kOutput, calls=%fused_computation.1 | convolution fusion | flops 4328488960 | bytes 33817600 | tf_op jit(solution)/shard_map/dot_general | solution.py:89
  730.8 31.7 %all_gather.6 = bf16[262144]{0:T(1024)(128)(2,1)S(1)} all-gather(bf16[32768]{0:T(1024)(128)(2,1)S(1)} %multiply_convert_fusion.1), channel_id=1, replica_groups=mesh['frag'=4,'band'=8] {'band'}, dimensions={0}, use_global_device_ids=true | all-gather | bytes 589824 | tf_op jit(solution)/shard_map/all_gather | solution.py:98
  762.6 0.4 reshape.255
  763.0 0.9 fusion.36
  764.2 9.2 dynamic_update_slice.3
  773.3 0.9 fusion.27
  774.3 32.7 %all-reduce.13.cloned.1.call-done = bf16[16,128,128]{2,1,0:T(8,128)(2,1)} async-done(((bf16[16,128,128]{2,1,0:T(8,128)(2,1)}), bf16[16,128,128]{2,1,0:T(8,128)(2,1)}) %all-reduce.13.cloned.1.call-update) | async-done | bytes 524304 | tf_op jit(solution)/shard_map/psum | solution.py:106
  806.9 1.9 fusion.40
  808.9 1.3 fusion.6
  810.2 1.1 copy.38
  811.3 5.5 all-to-all-start.2
  817.1 13.3 %all-to-all-done.2 = bf16[16,128,128]{2,0,1:T(8,128)(2,1)S(1)} async-done(((bf16[16,128,128]{2,0,1:T(8,128)(2,1)}), bf16[16,128,128]{2,0,1:T(8,128)(2,1)S(1)}, u32[]{:S(2)}, u32[]{:S(2)}) %all-to-all-start.2) | async-done | bytes 524320 | tf_op jit(solution)/shard_map/all_to_all | solution.py:110
  830.5 1.0 convolution_multiply_fusion
  831.5 1.3 fusion.44
  832.8 0.6 copy.44
  833.4 28.5 %all_to_all.72 = f32[128,16,128]{2,1,0:T(8,128)S(1)} all-to-all(f32[128,16,128]{2,1,0:T(8,128)S(1)} %copy.44), channel_id=1, replica_groups=mesh['frag'=4,'band'=8] {'band'}, dimensions={0} | all-to-all | bytes 2097152 | tf_op jit(solution)/shard_map/all_to_all | solution.py:121
  862.1 1.3 convolution_bitcast_fusion
  863.4 4.2 fusion.90
  869.4 6.0 all-to-all-start.1
  875.4 341.0 %all-gather.2.cloned.1.call-done = bf16[128,128,128]{2,1,0:T(8,128)(2,1)} async-done(((bf16[16,128,128]{2,1,0:T(8,128)(2,1)}), bf16[128,128,128]{2,1,0:T(8,128)(2,1)}) %all-gather.2.cloned.1.call-update) | async-done | bytes 4194320 | tf_op jit(solution)/shard_map/all_gather | solution.py:125
  1216.5 2.0 fusion.18
  1218.5 1.3 reshape.256
  1219.8 15.2 %and_select_fusion = f32[1,262144]{1,0:T(1,128)} fusion(f32[1,262144]{1,0:T(1,128)S(1)} %reshape.256, s32[]{:T(128)} %bitcast.2, s32[]{:T(128)} %bitcast.1, s32[]{:T(128)} %bitcast), kind=kLoop, calls=%fused_computation.9 | loop fusion | flops 9175040 | bytes 2097164 | tf_op jit(solution)/shard_map/mul | solution.py:132
  1235.0 52.8 %all-to-all-done.1 = bf16[8,32,32768]{2,1,0:T(8,128)(2,1)} async-done(((bf16[8,32,32768]{2,1,0:T(8,128)(2,1)}), bf16[8,32,32768]{2,1,0:T(8,128)(2,1)}, u32[]{:S(2)}, u32[]{:S(2)}) %all-to-all-start.1) | async-done | bytes 16777248 | tf_op jit(solution)/shard_map/all_to_all | solution.py:92
  1287.8 18.5 %copy.36 = bf16[32,8,32768]{2,1,0:T(8,128)(2,1)} copy(bf16[32,8,32768]{2,0,1:T(8,128)(2,1)} %bitcast.8) | data formatting | bytes 33554432 | tf_op jit(solution)/shard_map/all_to_all | solution.py:92
  1306.3 15.0 %broadcast_in_dim.4 = bf16[1,32,262144]{2,1,0:T(8,128)(2,1)} reshape(bf16[32,8,32768]{2,1,0:T(8,128)(2,1)} %copy.36) | data formatting | bytes 33554432 | tf_op jit(solution)/shard_map/broadcast_in_dim | solution.py:133
  (23 shorter events, 1.9 us)
Async XLA Ops:
  7.2 694.4 %all-reduce.11.cloned.1.call-start = ((), (), s32[]{:S(2)}) async-start(), calls=%async_computation.4 | async-start | bytes 524288 | tf_op jit(solution)/shard_map/psum | solution.py:87
  617.6 13.9 %copy-start = (s32[1,3]{1,0:T(1,128)S(1)}, s32[1,3]{1,0:T(1,128)}, u32[]{:S(2)}) copy-start(s32[1,3]{1,0:T(1,128)} %get-tuple-element.20) | copy-start | bytes 40
  617.6 17.7 %copy-start.2 = (s32[4]{0:T(128)S(1)}, s32[4]{0:T(128)}, u32[]{:S(2)}) copy-start(s32[4]{0:T(128)} %param.11) | copy-start | bytes 52
  617.6 96.9 %copy-start.1 = (f32[1,256]{1,0:T(1,128)S(1)}, f32[1,256]{1,0:T(1,128)}, u32[]{:S(2)}) copy-start(f32[1,256]{1,0:T(1,128)} %param.8) | copy-start | bytes 3076
  631.3 175.6 %all-reduce.13.cloned.1.call-start = ((), (), s32[]{:S(2)}) async-start(), calls=%async_computation.5 | async-start | bytes 1048576 | tf_op jit(solution)/shard_map/psum | solution.py:106
  811.3 19.0 %all-to-all-start.2 = ((bf16[16,128,128]{2,0,1:T(8,128)(2,1)}), bf16[16,128,128]{2,0,1:T(8,128)(2,1)S(1)}, u32[]{:S(2)}, u32[]{:S(2)}) async-start(bf16[16,128,128]{2,0,1:T(8,128)(2,1)} %copy.38), calls=%async_computation.2 | async-start | bytes 1048576 | tf_op jit(solution)/shard_map/all_to_all | solution.py:110
  816.8 399.6 %all-gather.2.cloned.1.call-start = ((), (), s32[]{:S(2)}) async-start(), calls=%async_computation.6 | async-start | bytes 4718592 | tf_op jit(solution)/shard_map/all_gather | solution.py:125
  869.4 418.4 %all-to-all-start.1 = ((bf16[8,32,32768]{2,1,0:T(8,128)(2,1)}), bf16[8,32,32768]{2,1,0:T(8,128)(2,1)}, u32[]{:S(2)}, u32[]{:S(2)}) async-start(bf16[8,32,32768]{2,1,0:T(8,128)(2,1)} %bitcast.107), calls=%async_computation.1 | async-start | bytes 33554432 | tf_op jit(solution)/shard_map/all_to_all | solution.py:92
Sparse Core Ops, SparseCore 0:
  631.4 70.0 all-reduce.10
  774.4 32.5 all-reduce.12
  867.8 348.6 all-gather.1
where the time goes:
time: 1340 us; the launch traced here: 1330 us
  waiting for transfers between devices  503 us (38%)
  blocking collectives  430 us (32%)
  local copies, waits for them, and re-layouts  190 us (14%)
  other arithmetic  119 us (9%)
  matrix products  51.4 us (4%)
  between operations  22.2 us (2%)
    all_to_all x1, blocking collectives, body(): lax.all_to_all(trial, 'band', split_axis=1, concat_axis=0, tiled=True)  370 us
    all_gather x1, waiting for transfers between devices, body(): lax.all_gather(total_potential.astype(jnp.bfloat16), 'band', axis=0, tile...  341 us
    slice x3, local copies, waits for them, and re-layouts, shifted(): return jnp.concatenate([field[:, offset:], tail], axis=1)  132 us
    convert_element_type x1, other arithmetic, body(): trial = (mask[None, :] * (waves - step_size * applied)).astype(jnp.bfloat16)  74.9 us
    psum x1, waiting for transfers between devices, body(): gram = lax.psum(partial_value, 'band') * cell_volume  63.6 us
    all_to_all x1, waiting for transfers between devices, body(): lax.all_to_all(fresh.astype(jnp.bfloat16), 'band', split_axis=0, concat_a...  52.8 us
    psum x1, waiting for transfers between devices, body(): patched = lax.psum(mine.astype(jnp.bfloat16), 'frag').astype(jnp.float32)  32.7 us
    all_gather x1, blocking collectives, body(): lax.all_gather(density.astype(jnp.bfloat16), 'band', axis=0, tiled=True)  31.7 us
  transfers between devices with their start and end apart: 5, of which 5 were waited for; matrix products, arithmetic and copies ran while one was open for 2% of the time, Pallas kernels for 0%

commit v1 on v0

--- a/solution.py
+++ b/solution.py
@@ -1,6 +1,10 @@
+import functools
+
 import jax
 import jax.numpy as jnp
 from jax import lax
+from jax.experimental import pallas as pl
+from jax.experimental.pallas import tpu as pltpu
 from jax.sharding import PartitionSpec as P
 
 NB = 256
@@ -44,12 +48,235 @@
     return (inverse_part / jnp.sqrt(frobenius)).astype(jnp.bfloat16)
 
 
-def shifted(field, offset):
-    if offset > 0:
-        tail = jnp.zeros((field.shape[0], offset), field.dtype)
-        return jnp.concatenate([field[:, offset:], tail], axis=1)
-    head = jnp.zeros((field.shape[0], -offset), field.dtype)
-    return jnp.concatenate([head, field[:, :offset]], axis=1)
+GROUP = 8 * BOX
+LANES = 128
+
+
+def step_plan(band_count):
+    return (2, 1) if 16 % band_count == 0 else (1, 2)
+
+
+def live_units(sizes, band_count):
+    planes, parts = step_plan(band_count)
+    unit = jnp.arange(BOX // planes * parts, dtype=jnp.int32)
+    per_device = sizes[0] * parts // (planes * band_count)
+    owner = jnp.minimum(unit // per_device, band_count - 1)
+    return (owner, unit % per_device)
+
+
+def trial_kernel(planes, parts, sizes, owner, local, prev, main, after, potential, out):
+    step, part = pl.program_id(0), pl.program_id(1)
+    size_x, size_y, size_z = sizes[0], sizes[1], sizes[2]
+    plane_cells = BOX * BOX
+    place = local[step * parts + part]
+    groups = size_y // (8 * parts)
+    rows = out.shape[1]
+    band_rows = min(rows, 16)
+    z = lax.rem(lax.broadcasted_iota(jnp.int32, (band_rows, LANES), 1), BOX)
+    low_half = lax.broadcasted_iota(jnp.int32, (band_rows, LANES), 1) < BOX
+    alive = z < size_z
+    has_up = z < size_z - 1
+    has_down = z > 0
+    weight = jnp.where(alive, 0.5 * step_size, 0.0)
+
+    @pl.when(step * planes < size_x)
+    def _():
+        for p in range(planes):
+            x = step * planes + p
+            below, below_at = (prev, 0) if p == 0 else (main, (p - 1) * plane_cells)
+            above, above_at = (after, 0) if p == planes - 1 else (main, (p + 1) * plane_cells)
+            below_on = jnp.where(x > 0, 1.0, 0.0)
+            above_on = jnp.where(x + 1 < size_x, 1.0, 0.0)
+
+            def group_step(local_group, carry):
+                group = part * groups + local_group
+                base = group * GROUP
+                target = ((place * planes + p) * groups + local_group) * (8 * size_z)
+                head_on = jnp.where(group > 0, 1.0, 0.0)
+                tail_on = jnp.where(group * 8 + 8 < size_y, 1.0, 0.0)
+                for first in range(0, rows, band_rows):
+                    band = slice(first, first + band_rows)
+
+                    def load(ref, at):
+                        return ref[band, pl.ds(pl.multiple_of(at, LANES), LANES)].astype(
+                            jnp.float32
+                        )
+
+                    def store(k, value):
+                        at = pl.multiple_of(target + k * LANES, LANES)
+                        out[0, band, pl.ds(at, LANES)] = value.astype(out.dtype)
+
+                    here = [load(main, p * plane_cells + base + k * LANES) for k in range(4)]
+                    head = load(main, p * plane_cells + jnp.maximum(base - LANES, 0)) * head_on
+                    tail = (
+                        load(main, p * plane_cells + jnp.minimum(base + GROUP, plane_cells - LANES))
+                        * tail_on
+                    )
+                    turned = [pltpu.roll(v, BOX, 1) for v in [head] + here + [tail]]
+                    trial = []
+                    for k in range(4):
+                        v = here[k]
+                        at = base + k * LANES
+                        beside = jnp.where(has_up, pltpu.roll(v, LANES - 1, 1), 0.0)
+                        beside = beside + jnp.where(has_down, pltpu.roll(v, 1, 1), 0.0)
+                        beside = beside + turned[k + 1]
+                        beside = beside + jnp.where(low_half, turned[k], turned[k + 2])
+                        beside = beside + below_on * load(below, below_at + at)
+                        beside = beside + above_on * load(above, above_at + at)
+                        pot = potential[
+                            0:1, pl.ds(pl.multiple_of(p * plane_cells + at, LANES), LANES)
+                        ]
+                        own = jnp.where(alive, (1.0 - 3.0 * step_size) - step_size * pot, 0.0)
+                        trial.append(own * v + weight * beside)
+
+                    @pl.when(size_z == 64)
+                    def _():
+                        for k in range(4):
+                            store(k, trial[k])
+
+                    @pl.when(size_z == 48)
+                    def _():
+                        for k in range(3):
+                            filler = pltpu.roll(trial[3], 48 - 16 * k, 1)
+                            store(k, jnp.where(z < 48, trial[k], filler))
+
+                    @pl.when(size_z == 32)
+                    def _():
+                        for k in range(2):
+                            filler = pltpu.roll(trial[2 * k + 1], 32, 1)
+                            store(k, jnp.where(z < 32, trial[2 * k], filler))
+
+                return carry
+
+            lax.fori_loop(0, groups, group_step, 0)
+
+
+def packed_trial(wave, potential, sizes, owner, local, width, band_count):
+    rows = wave.shape[0]
+    planes, parts = step_plan(band_count)
+    plane_cells = BOX * BOX
+
+    def plane(step, sizes, shift):
+        return jnp.clip(step * planes + shift, 0, sizes[0] - 1)
+
+    def whole(i, j, sizes, owner, local):
+        return (0, jnp.minimum(i, sizes[0] // planes - 1))
+
+    return pl.pallas_call(
+        functools.partial(trial_kernel, planes, parts),
+        out_shape=jax.ShapeDtypeStruct((band_count, rows, width), jnp.bfloat16),
+        grid_spec=pltpu.PrefetchScalarGridSpec(
+            num_scalar_prefetch=3,
+            grid=(BOX // planes, parts),
+            in_specs=[
+                pl.BlockSpec((rows, plane_cells), lambda i, j, s, o, l: (0, plane(i, s, -1))),
+                pl.BlockSpec((rows, planes * plane_cells), whole),
+                pl.BlockSpec((rows, plane_cells), lambda i, j, s, o, l: (0, plane(i, s, planes))),
+                pl.BlockSpec((1, planes * plane_cells), whole),
+            ],
+            out_specs=pl.BlockSpec(
+                (1, rows, width), lambda i, j, s, o, l: (o[i * parts + j], 0, 0)
+            ),
+        ),
+        compiler_params=pltpu.CompilerParams(vmem_limit_bytes=40 << 20),
+        name="packed_trial",
+    )(sizes, owner, local, wave, wave, wave, potential)
+
+
+def unpack_kernel(planes, parts, sizes, owner, local, packed, out):
+    step, part = pl.program_id(0), pl.program_id(1)
+    size_x, size_y, size_z = sizes[0], sizes[1], sizes[2]
+    plane_cells = BOX * BOX
+    place = local[step * parts + part]
+    groups = size_y // (8 * parts)
+    rows = out.shape[0]
+    band_rows = min(rows, 16)
+    z = lax.rem(lax.broadcasted_iota(jnp.int32, (band_rows, LANES), 1), BOX)
+
+    @pl.when((part == 0) & ((size_y < BOX) | (step * planes >= size_x)))
+    def _():
+        def clear(k, carry):
+            out[:, pl.ds(pl.multiple_of(k * GROUP, GROUP), GROUP)] = jnp.zeros(
+                (rows, GROUP), out.dtype
+            )
+            return carry
+
+        lax.fori_loop(0, planes * plane_cells // GROUP, clear, 0)
+
+    @pl.when(step * planes < size_x)
+    def _():
+        for p in range(planes):
+
+            def group_step(local_group, carry):
+                base = p * plane_cells + (part * groups + local_group) * GROUP
+                source = ((place * planes + p) * groups + local_group) * (8 * size_z)
+                for first in range(0, rows, band_rows):
+                    band = slice(first, first + band_rows)
+
+                    def load(k):
+                        at = pl.multiple_of(source + k * LANES, LANES)
+                        return packed[0, band, pl.ds(at, LANES)].astype(jnp.float32)
+
+                    def store(k, value):
+                        at = pl.multiple_of(base + k * LANES, LANES)
+                        out[band, pl.ds(at, LANES)] = value.astype(out.dtype)
+
+                    @pl.when(size_z == 64)
+                    def _():
+                        for k in range(4):
+                            store(k, load(k))
+
+                    @pl.when(size_z == 48)
+                    def _():
+                        last = jnp.zeros((band_rows, LANES), jnp.float32)
+                        for k in range(3):
+                            value = load(k)
+                            store(k, jnp.where(z < 48, value, 0.0))
+                            mine = (z >= 16 * k) & (z < 16 * k + 16)
+                            last = jnp.where(mine, pltpu.roll(value, 80 + 16 * k, 1), last)
+                        store(3, last)
+
+                    @pl.when(size_z == 32)
+                    def _():
+                        for k in range(2):
+                            value = load(k)
+                            store(2 * k, jnp.where(z < 32, value, 0.0))
+                            store(2 * k + 1, jnp.where(z < 32, pltpu.roll(value, 96, 1), 0.0))
+
+                return carry
+
+            lax.fori_loop(0, groups, group_step, 0)
+
+
+def unpacked(packed, sizes, owner, local):
+    band_count, rows, width = packed.shape
+    planes, parts = step_plan(band_count)
+    return pl.pallas_call(
+        functools.partial(unpack_kernel, planes, parts),
+        out_shape=jax.ShapeDtypeStruct((rows, BOX**3), packed.dtype),
+        grid_spec=pltpu.PrefetchScalarGridSpec(
+            num_scalar_prefetch=3,
+            grid=(BOX // planes, parts),
+            in_specs=[
+                pl.BlockSpec((1, rows, width), lambda i, j, s, o, l: (o[i * parts + j], 0, 0))
+            ],
+            out_specs=pl.BlockSpec((rows, planes * BOX * BOX), lambda i, j, s, o, l: (0, i)),
+        ),
+        compiler_params=pltpu.CompilerParams(vmem_limit_bytes=40 << 20),
+        name="unpacked",
+    )(sizes, owner, local, packed)
+
+
+def summed(partial_value, band_count):
+    blocks = partial_value.reshape(band_count, NB // band_count, NB)
+    blocks = lax.all_to_all(blocks, "band", split_axis=0, concat_axis=0, tiled=True)
+    mine = jnp.sum(blocks, axis=0)
+    return gathered(mine, band_count).reshape(NB, NB)
+
+
+def gathered(block, band_count):
+    copies = jnp.broadcast_to(block[None], (band_count,) + block.shape)
+    return lax.all_to_all(copies, "band", split_axis=0, concat_axis=0, tiled=True)
 
 
 def body(wave_coeffs, old_potential, occupations, box_sizes, box_offsets, patch_signs):
@@ -70,34 +297,56 @@
     mask = (
         (x_coord < sizes_here[0]) & (y_coord < sizes_here[1]) & (z_coord < sizes_here[2])
     ).astype(jnp.float32)
-    waves = wave_coeffs[0].astype(jnp.float32) * mask[None, :]
-    beside = shifted(waves, 1) * (z_coord < BOX - 1).astype(jnp.float32)[None, :]
-    beside = beside + shifted(waves, -1) * (z_coord > 0).astype(jnp.float32)[None, :]
-    beside = beside + shifted(waves, BOX) * (y_coord < BOX - 1).astype(jnp.float32)[None, :]
-    beside = beside + shifted(waves, -BOX) * (y_coord > 0).astype(jnp.float32)[None, :]
-    beside = beside + shifted(waves, BOX * BOX) * (x_coord < BOX - 1).astype(jnp.float32)[None, :]
-    beside = beside + shifted(waves, -BOX * BOX) * (x_coord > 0).astype(jnp.float32)[None, :]
-    kinetic = 6.0 * waves - beside
-    applied = 0.5 * kinetic + old_potential[0][None, :] * waves
-    trial = (mask[None, :] * (waves - step_size * applied)).astype(jnp.bfloat16)
-    cell_rows = lax.all_to_all(trial, "band", split_axis=1, concat_axis=0, tiled=True)
-    partial_value = lax.dot_general(
-        cell_rows, cell_rows, (((1,), (1,)), ((), ())), preferred_element_type=jnp.float32
-    )
-    gram = lax.psum(partial_value, "band") * cell_volume
+    owner, local = live_units(sizes_here, band_count)
+    room = cells // band_count
+    lengths = (BOX // 2, BOX * 3 // 4, BOX)
+    widths = sorted({a * b * c // band_count for a in lengths for b in lengths for c in lengths})
+    width_here = sizes_here[0] * sizes_here[1] * sizes_here[2] // band_count
+    choice = jnp.sum((width_here > jnp.array(widths)).astype(jnp.int32))
+
+    def forward(width):
+        def branch(wave, potential):
+            trial = packed_trial(wave, potential, sizes_here, owner, local, width, band_count)
+            rows = lax.all_to_all(trial, "band", split_axis=0, concat_axis=0, tiled=True)
+            rows = rows.reshape(NB, width)
+            partial_value = lax.dot_general(
+                rows, rows, (((1,), (1,)), ((), ())), preferred_element_type=jnp.float32
+            )
+            return (jnp.pad(rows, ((0, 0), (0, room - width))), partial_value)
+
+        return branch
+
+    cell_rows, partial_value = lax.switch(
+        choice, [forward(width) for width in widths], wave_coeffs[0], old_potential
+    )
+    gram = summed(partial_value, band_count) * cell_volume
     coeff = newton_schulz(gram)
-    fresh = lax.dot_general(
-        coeff, cell_rows, (((0,), (0,)), ((), ())), preferred_element_type=jnp.float32
-    )
-    waves_out = lax.all_to_all(
-        fresh.astype(jnp.bfloat16), "band", split_axis=0, concat_axis=1, tiled=True
-    )
-    density = jnp.sum(occupations[0][:, None] * fresh * fresh, axis=0) / NB
+
+    def backward(width):
+        def branch(cell_rows, coeff):
+            fresh = lax.dot_general(
+                coeff,
+                cell_rows[:, :width],
+                (((0,), (0,)), ((), ())),
+                preferred_element_type=jnp.float32,
+            )
+            density = jnp.sum(occupations[0][:, None] * fresh * fresh, axis=0) / NB
+            sent = fresh.astype(jnp.bfloat16).reshape(band_count, NB // band_count, width)
+            back = lax.all_to_all(sent, "band", split_axis=0, concat_axis=0, tiled=True)
+            return (
+                unpacked(back, sizes_here, owner, local),
+                jnp.pad(density.astype(jnp.bfloat16), (0, room - width)),
+            )
+
+        return branch
+
+    waves_out, density = lax.switch(
+        choice, [backward(width) for width in widths], cell_rows, coeff
+    )
     slab_rows = G // band_count
     slab_start = band_index * slab_rows
-    whole_box = lax.all_gather(density.astype(jnp.bfloat16), "band", axis=0, tiled=True).astype(
-        density.dtype
-    )
+    boxes = gathered(density, band_count).astype(jnp.float32)
+    whole_box = unpacked(boxes[:, None, :], sizes_here, owner, local)
     padded_x = jnp.pad(whole_box.reshape(BOX, BOX, BOX), ((G, G), (0, 0), (0, 0)))
     planes = lax.dynamic_slice_in_dim(padded_x, slab_start - offsets_here[0] + G, slab_rows, 0)
     frame = jnp.zeros((slab_rows, G + BOX, G + BOX), jnp.float32)

time: 1340 us -> 914 us (0.68)
  waiting for transfers between devices: 503 us -> 303 us
  Pallas kernels: 0 us -> 170 us
  local copies, waits for them, and re-layouts: 190 us -> 20.6 us
  blocking collectives: 430 us -> 273 us
  other arithmetic: 119 us -> 34.6 us
    all_gather x1, waiting for transfers between devices: 341 us -> 69.9 us  [body(): lax.all_gather(total_potential.astype(jnp.bfloat16), 'band', axis=0, tile...]
    pallas_call x0 -> x3, Pallas kernels: none -> 170 us  [the longest x1 118 us: packed_trial(): pl.pallas_call(functools.partial(trial_kernel, planes, parts), out_shape=...]
    all_to_all x1 -> x2, waiting for transfers between devices: 52.8 us -> 188 us  [the longest x1 185 us: branch(): back = lax.all_to_all(sent, 'band', split_axis=0, concat_axis=0, tiled=True)]
    slice x4 -> x1, local copies, waits for them, and re-layouts: 132 us -> 0.66 us  [body(): width_here = sizes_here[0] * sizes_here[1] * sizes_here[2] // band_count]
    all_to_all x1 -> x3, blocking collectives: 370 us -> 244 us  [the longest x1 222 us: branch(): lax.all_to_all(trial, 'band', split_axis=0, concat_axis=0, tiled=True)]
    convert_element_type x6 -> x2, other arithmetic: 80.4 us -> 1.09 us  [the longest x1 1.08 us: body(): boxes = gathered(density, band_count).astype(jnp.float32)]
    psum x1 -> x0, waiting for transfers between devices: 63.6 us -> none  [body(): gram = lax.psum(partial_value, 'band') * cell_volume]
    all_gather x1 -> x0, blocking collectives: 31.7 us -> none  [body(): lax.all_gather(density.astype(jnp.bfloat16), 'band', axis=0, tiled=True)]
  transfers between devices with their start and end apart: 5 -> 5, of which waited for: 5 -> 5; matrix products, arithmetic and copies ran while one was open for 2% -> 0% of each run, Pallas kernels for 0% -> 0%
where the time goes in v1:
time: 914 us; the launch traced here: 903 us
  waiting for transfers between devices  303 us (33%)
  blocking collectives  273 us (30%)
  Pallas kernels  170 us (19%)
  matrix products  47.7 us (5%)
  other arithmetic  34.6 us (4%)
  between operations  27.4 us (3%)
  local copies, waits for them, and re-layouts  20.6 us (2%)
  starting transfers between devices  15.2 us (2%)
  loops' own time  11.6 us (1%)
    all_to_all x1, blocking collectives, branch(): lax.all_to_all(trial, 'band', split_axis=0, concat_axis=0, tiled=True)  222 us
    all_to_all x1, waiting for transfers between devices, branch(): back = lax.all_to_all(sent, 'band', split_axis=0, concat_axis=0, tiled=True)  185 us
    pallas_call x1, Pallas kernels, packed_trial(): pl.pallas_call(functools.partial(trial_kernel, planes, parts), out_shape=...  118 us
    all_gather x1, waiting for transfers between devices, body(): lax.all_gather(total_potential.astype(jnp.bfloat16), 'band', axis=0, tile...  69.9 us
    pallas_call x2, Pallas kernels, unpacked(): pl.pallas_call(functools.partial(unpack_kernel, planes, parts), out_shape...  52 us
    psum x1, waiting for transfers between devices, body(): patched = lax.psum(mine.astype(jnp.bfloat16), 'frag').astype(jnp.float32)  31.7 us
    all_to_all x1, blocking collectives, body(): lax.all_to_all(columns, 'band', split_axis=0, concat_axis=1, tiled=True)  28.5 us
  transfers between devices with their start and end apart: 5, of which 5 were waited for; matrix products, arithmetic and copies ran while one was open for 0% of the time, Pallas kernels for 0%

profile of v1, /device:TPU:0, one launch (start us, length us, event | category | flops | bytes accessed | tf_op | source)
XLA Modules:
  0.0 902.8 jit_solution(14133066302141322945)
XLA Ops:
  7.2 0.7 copy-done
  7.9 0.7 fusion.100
  12.7 1.3 fusion.75
  14.8 353.7 %conditional.2 = (bf16[256,32768]{1,0:T(8,128)(2,1)}, f32[256,256]{1,0:T(8,128)S(1)}) conditional(s32[]{:T(128)} %clamp.4, (s32[3]{0:T(128)S(1)}, s32[32]{0:T(128)S(1)}, s32[32]{0:T(128)S(1)}, bf16[32,262144]{1,0:T(8,128)(2,1)}, f32[1,262144]{1,0:T(1,128)}) %tuple.143, (s32[3]{0:T(128)S(1)}, s32[32]{0:T(128)S(1)}, ...), branch_computations={%region_1.2_spmd, %region_2.3_spmd, %region_3.4_spmd, %region_4.5_... | conditional | flops 4294967296 | bytes 67371024 | solution.py:319
  15.2 118.4 %packed_trial.19 = bf16[8,32,32768]{2,1,0:T(8,128)(2,1)} custom-call(s32[3]{0:T(128)S(1)} %get-tuple-element.266.sizes, s32[32]{0:T(128)S(1)} %get-tuple-element.267.owner, s32[32]{0:T(128)S(1)} %get-tuple-element.268.local, bf16[32,262144]{1,0:T(8,128)(2,1)} %get-tuple-element.269.prev.main.after, bf16[32,262144]{1,0:T(8,128)(2,1)} %get-tuple-element.269.prev.main.after, ...), custom_call_target="tpu_custom_call" | custom-call | tf_op jit(solution)/shard_map/cond/branch_9_fun/packed_trial/pallas_call | solution.py:165
  133.6 221.8 %all_to_all.141 = bf16[8,32,32768]{2,1,0:T(8,128)(2,1)} all-to-all(bf16[8,32,32768]{2,1,0:T(8,128)(2,1)} %packed_trial.19), channel_id=1, replica_groups=mesh['frag'=4,'band'=8] {'band'}, dimensions={0} | all-to-all | bytes 33554432 | tf_op jit(solution)/shard_map/cond/branch_9_fun/all_to_all | solution.py:310
  355.4 12.9 %fusion.111 = f32[256,256]{1,0:T(8,128)S(1)} fusion(bf16[256,32768]{1,0:T(8,128)(2,1)} %bitcast.9), kind=kOutput, calls=%fused_computation.172 | convolution fusion | flops 4294967296 | bytes 17039360 | tf_op jit(solution)/shard_map/cond/branch_9_fun/dot_general | solution.py:312
  368.5 11.3 %all_to_all.142 = f32[8,32,256]{2,1,0:T(8,128)S(1)} all-to-all(f32[8,32,256]{2,1,0:T(8,128)S(1)} %bitcast.206), channel_id=1, replica_groups=mesh['frag'=4,'band'=8] {'band'}, dimensions={0} | all-to-all | bytes 524288 | tf_op jit(solution)/shard_map/all_to_all | solution.py:272
  379.8 10.9 %all_to_all.143 = f32[8,32,256]{2,1,0:T(8,128)S(1)} all-to-all(f32[8,32,256]{2,1,0:T(8,128)S(1)} %broadcast_in_dim.53), channel_id=1, replica_groups=mesh['frag'=4,'band'=8] {'band'}, dimensions={0} | all-to-all | bytes 524288 | tf_op jit(solution)/shard_map/all_to_all | solution.py:279
  390.8 0.7 multiply_reduce_fusion
  392.7 0.4 fusion.112
  393.1 0.4 fusion.35
  393.5 0.4 fusion.113
  394.3 0.4 fusion.34
  394.7 0.4 fusion.115
  395.1 0.4 fusion.116
  395.4 0.4 fusion.33
  395.8 0.4 fusion.117
  396.6 0.4 fusion.32
  397.8 0.4 fusion.31
  398.1 0.4 fusion.121
  398.9 0.4 fusion.30
  399.3 0.4 fusion.123
  399.7 0.4 fusion.124
  400.1 0.4 fusion.29
  400.5 0.4 fusion.37
  400.9 255.7 %conditional.3 = (bf16[32768]{0:T(1024)(128)(2,1)S(1)}, bf16[1,32,262144]{2,1,0:T(8,128)(2,1)}) conditional(s32[]{:T(128)} %clamp.4, (f32[1,256]{1,0:T(1,128)S(1)}, bf16[256,32768]{1,0:T(8,128)(2,1)}, bf16[256,256]{1,0:T(8,128)(2,1)S(1)}, s32[3]{0:T(128)S(1)}, s32[32]{0:T(128)S(1)}, ...), branch_computations={%region_13.15_spmd, %region_15.17_spmd, %region_17.19_spmd, %regio... | conditional | flops 4328554496 | bytes 84345904 | solution.py:343
  411.5 16.3 %fusion.98 = (bf16[256,32768]{1,0:T(8,128)(2,1)}, f32[32768]{0:T(1024)S(1)}) fusion(f32[256]{0:T(256)S(1)} %bitcast.217, bf16[256,256]{1,0:T(8,128)(2,1)S(1)} %get-tuple-element.326, bf16[256,32768]{1,0:T(8,128)(2,1)} %get-tuple-element.327), kind=kOutput, calls=%fused_computation.159 | convolution fusion | flops 4328488960 | bytes 33817600 | tf_op jit(solution)/shard_map/cond/branch_9_fun/dot_general | solution.py:327
  427.7 5.7 all-to-all-start.19
  433.5 184.9 %all-to-all-done.19.packed = bf16[8,32,32768]{2,1,0:T(8,128)(2,1)} async-done(((bf16[8,32,32768]{2,1,0:T(8,128)(2,1)}), bf16[8,32,32768]{2,1,0:T(8,128)(2,1)}, u32[]{:S(2)}, u32[]{:S(2)}) %all-to-all-start.19) | async-done | bytes 16777248 | tf_op jit(solution)/shard_map/cond/branch_9_fun/all_to_all | solution.py:335
  618.4 37.8 %unpacked.20 = bf16[32,262144]{1,0:T(8,128)(2,1)} custom-call(s32[3]{0:T(128)S(1)} %get-tuple-element.328.sizes, s32[32]{0:T(128)S(1)} %get-tuple-element.329.owner, s32[32]{0:T(128)S(1)} %get-tuple-element.330.local, bf16[8,32,32768]{2,1,0:T(8,128)(2,1)} %all-to-all-done.19.packed), custom_call_target="tpu_custom_call" | custom-call | tf_op jit(solution)/shard_map/cond/branch_9_fun/unpacked/pallas_call | solution.py:254
  656.7 0.5 broadcast_in_dim.55
  657.2 0.5 broadcast.405
  657.7 3.9 reduce.5
  661.7 1.2 reshape.319
  662.9 3.5 all-to-all-start.22
  666.6 0.7 constant_dynamic-slice_fusion
  667.3 0.7 fusion.99
  671.2 0.6 dynamic_slice.21
  673.6 2.9 all-to-all-done.22
  676.6 0.5 reshape.320
  677.1 1.1 convert_element_type.175.packed
  678.2 14.3 %unpacked.21 = f32[1,262144]{1,0:T(1,128)S(1)} custom-call(s32[3]{0:T(128)S(1)} %fusion.205.sizes, s32[32]{0:T(128)S(1)} %get-tuple-element.371.owner, s32[32]{0:T(128)S(1)} %get-tuple-element.370.local, f32[8,1,32768]{2,1,0:T(1,128)S(1)} %convert_element_type.175.packed), custom_call_target="tpu_custom_call" | custom-call | tf_op jit(solution)/shard_map/unpacked/pallas_call | solution.py:254
  692.5 0.5 broadcast.404
  693.0 9.3 %reduce.4 = f32[262144]{0:T(1024)S(1)} reduce(f32[1,262144]{1,0:T(1,128)S(1)} %unpacked.21, f32[]{:T(128)} %broadcast.404), dimensions={0}, to_apply=%pallas_call.63.reduce_sub_computation.3 | reduce | bytes 2097156 | tf_op jit(solution)/shard_map/unpacked/pallas_call | solution.py:254
  702.7 0.9 pad_dynamic-slice_fusion.1
  703.8 9.2 %dynamic_update_slice.3 = f32[16,192,192]{2,1,0:T(8,128)S(1)} dynamic-update-slice(f32[16,192,192]{2,1,0:T(8,128)S(1)} %broadcast_in_dim.54, f32[16,64,64]{2,1,0:T(8,128)} %pad_dynamic-slice_fusion.1, s32[]{:T(128)} %constant.228.clone.1, s32[]{:T(128)S(6)} %select_n.102, s32[]{:T(128)S(6)} %select_n.103) | dynamic-update-slice | bytes 524292 | tf_op jit(solution)/shard_map/dynamic_update_slice | solution.py:353
  713.0 0.9 fusion.40
  713.9 31.7 %all-reduce.22.cloned.1.call-done = bf16[16,128,128]{2,1,0:T(8,128)(2,1)} async-done(((bf16[16,128,128]{2,1,0:T(8,128)(2,1)}), bf16[16,128,128]{2,1,0:T(8,128)(2,1)}) %all-reduce.22.cloned.1.call-update) | async-done | bytes 524304 | tf_op jit(solution)/shard_map/psum | solution.py:355
  745.6 1.9 fusion.44
  747.5 1.3 fusion.28
  748.9 1.1 copy.34
  750.0 5.5 all-to-all-start.23
  756.0 13.1 %all-to-all-done.23 = bf16[16,128,128]{2,0,1:T(8,128)(2,1)S(1)} async-done(((bf16[16,128,128]{2,0,1:T(8,128)(2,1)}), bf16[16,128,128]{2,0,1:T(8,128)(2,1)S(1)}, u32[]{:S(2)}, u32[]{:S(2)}) %all-to-all-start.23) | async-done | bytes 524320 | tf_op jit(solution)/shard_map/all_to_all | solution.py:359
  769.2 1.0 convolution_multiply_fusion
  770.2 1.3 fusion.48
  771.5 0.6 copy.40
  772.1 28.5 %all_to_all.144 = f32[128,16,128]{2,1,0:T(8,128)S(1)} all-to-all(f32[128,16,128]{2,1,0:T(8,128)S(1)} %copy.40), channel_id=1, replica_groups=mesh['frag'=4,'band'=8] {'band'}, dimensions={0} | all-to-all | bytes 2097152 | tf_op jit(solution)/shard_map/all_to_all | solution.py:370
  800.8 1.3 convolution_bitcast_fusion
  802.1 3.2 fusion.101
  807.4 69.9 %all-gather.2.cloned.1.call-done = bf16[128,128,128]{2,1,0:T(8,128)(2,1)} async-done(((bf16[16,128,128]{2,1,0:T(8,128)(2,1)}), bf16[128,128,128]{2,1,0:T(8,128)(2,1)}) %all-gather.2.cloned.1.call-update) | async-done | bytes 4194320 | tf_op jit(solution)/shard_map/all_gather | solution.py:374
  877.3 2.0 fusion.38
  879.4 1.3 reshape.304
  880.7 15.1 %and_select_fusion = f32[1,262144]{1,0:T(1,128)} fusion(f32[1,262144]{1,0:T(1,128)S(1)} %reshape.304, s32[]{:T(128)} %bitcast.42, s32[]{:T(128)} %bitcast.41, s32[]{:T(128)} %bitcast.40), kind=kLoop, calls=%fused_computation.52 | loop fusion | flops 9175040 | bytes 2097164 | tf_op jit(solution)/shard_map/mul | solution.py:381
  (35 shorter events, 4.3 us)
Async XLA Ops:
  7.2 0.7 copy-start
  379.8 21.1 %copy-start.3 = (f32[1,256]{1,0:T(1,128)S(1)}, f32[1,256]{1,0:T(1,128)}, u32[]{:S(2)}) copy-start(f32[1,256]{1,0:T(1,128)} %param.29) | copy-start | bytes 3076
  400.9 270.3 %copy-start.4 = (s32[4]{0:T(128)S(1)}, s32[4]{0:T(128)}, u32[]{:S(2)}) copy-start(s32[4]{0:T(128)} %param.32) | copy-start | bytes 52
  427.7 190.7 %all-to-all-start.19 = ((bf16[8,32,32768]{2,1,0:T(8,128)(2,1)}), bf16[8,32,32768]{2,1,0:T(8,128)(2,1)}, u32[]{:S(2)}, u32[]{:S(2)}) async-start(bf16[8,32,32768]{2,1,0:T(8,128)(2,1)} %bitcast.187), calls=%async_computation.19 | async-start | bytes 33554432 | tf_op jit(solution)/shard_map/cond/branch_9_fun/all_to_all | solution.py:335
  662.9 13.7 %all-to-all-start.22 = ((bf16[8,2,16384]{2,1,0:T(2,128)(2,1)}), bf16[8,2,16384]{2,1,0:T(2,128)(2,1)S(1)}, u32[]{:S(2)}, u32[]{:S(2)}) async-start(bf16[8,2,16384]{2,1,0:T(2,128)(2,1)} %reshape.319), calls=%async_computation.22 | async-start | bytes 1048576 | tf_op jit(solution)/shard_map/all_to_all | solution.py:279
  666.4 79.3 %all-reduce.22.cloned.1.call-start = ((), (), s32[]{:S(2)}) async-start(), calls=%async_computation.25 | async-start | bytes 1048576 | tf_op jit(solution)/shard_map/psum | solution.py:355
  748.9 53.3 %copy-start.2 = (bf16[16,128,128]{2,1,0:T(8,128)(2,1)S(1)}, bf16[16,128,128]{2,1,0:T(8,128)(2,1)}, u32[]{:S(2)}) copy-start(bf16[16,128,128]{2,1,0:T(8,128)(2,1)} %all-reduce.22.cloned.1.call-done) | copy-start | bytes 1572868
  750.0 19.0 %all-to-all-start.23 = ((bf16[16,128,128]{2,0,1:T(8,128)(2,1)}), bf16[16,128,128]{2,0,1:T(8,128)(2,1)S(1)}, u32[]{:S(2)}, u32[]{:S(2)}) async-start(bf16[16,128,128]{2,0,1:T(8,128)(2,1)} %copy.34), calls=%async_computation.23 | async-start | bytes 1048576 | tf_op jit(solution)/shard_map/all_to_all | solution.py:359
  755.5 121.8 %all-gather.2.cloned.1.call-start = ((), (), s32[]{:S(2)}) async-start(), calls=%async_computation.26 | async-start | bytes 4718592 | tf_op jit(solution)/shard_map/all_gather | solution.py:374
  800.7 95.0 %copy-start.1 = (s32[4,3]{1,0:T(4,128)S(1)}, s32[4,3]{1,0:T(4,128)}, u32[]{:S(2)}) copy-start(s32[4,3]{1,0:T(4,128)} %param.30) | copy-start | bytes 148
Sparse Core Ops, SparseCore 0:
  714.0 31.5 all-reduce.21
  805.5 71.7 all-gather.1
